TPU v7x, 32 devices: a whole 2x2x4 slice. The times are simulated.
32 devices in a mesh: subtree: 8 (over z, core), front: 4 (over y, x).
Axes of the slice: x: 2, y: 2, z: 4, core: 2. Of those that a mesh axis runs over, the one named last changes fastest.
Arguments:
- leaf_rhs: float32 [8, 2048, 256], P('subtree', 'front'), may hold values from -6 to 6
- mid_rhs: float32 [2, 4096, 256], P(None, 'front'), may hold values from -6 to 6
- root_rhs: float32 [10240, 256], P('front'), may hold values from -6 to 6
- leaf_lower: float32 [8, 2048, 2048], P('subtree', None, 'front'), may hold values from -0.125 to 0.125
- leaf_below: float32 [8, 2048, 2048], P('subtree', None, 'front'), may hold values from -0.125 to 0.125
- leaf_right: float32 [8, 2048, 2048], P('subtree', None, 'front'), may hold values from -0.125 to 0.125
- leaf_upper: float32 [8, 2048, 2048], P('subtree', None, 'front'), may hold values from -0.125 to 0.125
- mid_lower: float32 [2, 4096, 4096], P(None, 'subtree', 'front'), may hold values from -0.09375 to 0.09375
- mid_below: float32 [2, 4096, 4096], P(None, 'front', 'subtree'), may hold values from -0.09375 to 0.09375
- mid_right: float32 [2, 4096, 4096], P(None, 'subtree', 'front'), may hold values from -0.09375 to 0.09375
- mid_upper: float32 [2, 4096, 4096], P(None, 'front', 'subtree'), may hold values from -0.09375 to 0.09375
- root_lower: float32 [10240, 10240], P('subtree', 'front'), may hold values from -0.0625 to 0.0625
- root_upper: float32 [10240, 10240], P('front', 'subtree'), may hold values from -0.0625 to 0.0625
- leaf_parent: int32 [8], replicated, may hold values from 0 to 1, as said below
- leaf_sizes: int32 [8], replicated, may hold values from 1024 to 2048, as said below
- leaf_map: int32 [8, 16], replicated, may hold values from 0 to 63, as said below
- mid_map: int32 [2, 32], replicated, may hold values from 0 to 79, as said below
Outputs:
- leaf_sol: float32 [8, 2048, 256], P('subtree', 'front')
- mid_sol: float32 [2, 4096, 256], P(None, 'front')
- root_sol: float32 [10240, 256], P('front')
Inputs may be any that keep to these rules, and one draw needn't show every extreme that they name: `leaf_parent`: every level-1 front is the parent of at least one lowest-level front. `leaf_sizes`: a multiple of 128; some front has all 2048 rows live. `leaf_map`: a front's blocks go to distinct parent blocks; update block b of a lowest-level front, with c = b // 4, goes to c * 8 + i or to that plus 4096 / 128, for some i with 0 <= i < 8. `mid_map`: a front's blocks go to distinct root blocks; update block b of a level-1 front, with c = b // 8, goes to c * 20 + i for some i with 0 <= i < 20.
All inputs are finite; a program needn't handle non-finite values.
Results may differ from a plain program's by a relative error of at most 0.00013.
Values sent between devices are 32-bit elements; how exact they have to be, the bound alone decides.
No kernel may reach another device: no remote copies, remote signals or barrier semaphores. Data moves between devices by JAX's collectives and lax.ppermute only.
A program may use at most 128 MiB of HBM per device.

v0:
```python
import jax
import jax.numpy as jnp
from jax import lax
from jax.sharding import PartitionSpec as P

MID_PIV = 4096
BLOCK = 128


def leaf_product(matrix, vector):
    return lax.psum_scatter(
        jnp.dot(
            matrix, vector, preferred_element_type=jnp.float32, precision=lax.Precision.HIGHEST
        ),
        "front",
        scatter_dimension=0,
        tiled=True,
    )


def across_front(partial_value):
    return lax.psum(partial_value, "front")


def across_subtree(partial_value):
    return lax.psum(partial_value, "subtree")


def batched(matrix, vector):
    return jnp.einsum(
        "fab,fbr->far",
        matrix,
        vector,
        preferred_element_type=jnp.float32,
        precision=lax.Precision.HIGHEST,
    )


def leaf_select(parents, blocks, fronts, column, width):
    front_ids = jnp.arange(fronts, dtype=jnp.int32)[:, None, None, None, None]
    halves = jnp.arange(2, dtype=jnp.int32)[None, :, None, None, None]
    slots = jnp.arange(width, dtype=jnp.int32)[None, None, :, None, None]
    target = halves * (MID_PIV // BLOCK) + column * width + slots
    match_parent = parents[None, None, None, :, None] == front_ids
    match_block = blocks[None, None, None, :, :] == target
    return (match_parent & match_block).astype(jnp.float32)


def on_device(
    leaf_rhs,
    mid_rhs,
    root_rhs,
    leaf_lower,
    leaf_below,
    leaf_right,
    leaf_upper,
    mid_lower,
    mid_below,
    mid_right,
    mid_upper,
    root_lower,
    root_upper,
    leaf_parent,
    leaf_sizes,
    leaf_map,
    mid_map,
):
    group = lax.axis_index("subtree")
    column = lax.axis_index("front")
    local_rows = leaf_rhs.shape[1]
    scenarios = leaf_rhs.shape[2]
    leaf_width = local_rows // BLOCK
    fronts = mid_rhs.shape[0]
    mid_width = mid_rhs.shape[1] // BLOCK
    root_width = root_rhs.shape[0] // BLOCK
    own_size = lax.dynamic_slice_in_dim(leaf_sizes, group, 1)
    positions = column * local_rows + jnp.arange(local_rows, dtype=jnp.int32)
    live = (positions < own_size[0]).astype(jnp.float32)[:, None]
    leaf_fwd = live * leaf_product(leaf_lower[0], live * leaf_rhs[0])
    leaf_contrib = -leaf_product(leaf_below[0], leaf_fwd)
    own_parent = lax.dynamic_slice_in_dim(leaf_parent, group, 1)
    own_blocks = lax.dynamic_slice(leaf_map, (group, column * leaf_width), (1, leaf_width))
    own_select = leaf_select(own_parent, own_blocks, fronts, column, mid_width)
    column_blocks = lax.dynamic_slice_in_dim(leaf_map, column * leaf_width, leaf_width, 1)
    selection = leaf_select(leaf_parent, column_blocks, fronts, column, mid_width)
    piece = lax.all_gather(leaf_contrib[None], "subtree", axis=0, tiled=True)
    shaped = piece.reshape(piece.shape[0], leaf_width, BLOCK, scenarios)
    assembled = jnp.einsum(
        "phqgk,gkbr->phqbr",
        selection,
        shaped,
        preferred_element_type=jnp.float32,
        precision=lax.Precision.HIGHEST,
    )
    mid_pivot = mid_rhs + assembled[:, 0].reshape(fronts, mid_width * BLOCK, scenarios)
    mid_update = assembled[:, 1].reshape(fronts, mid_width * BLOCK, scenarios)
    mid_fwd = across_front(batched(mid_lower, mid_pivot))
    mid_contrib = mid_update - across_subtree(batched(mid_below, mid_fwd))
    column_map = lax.dynamic_slice_in_dim(mid_map, column * mid_width, mid_width, 1)
    slots = jnp.arange(root_width, dtype=jnp.int32)[:, None, None]
    root_select = (column_map[None, :, :] == column * root_width + slots).astype(jnp.float32)
    root_added = jnp.einsum(
        "qpk,pkbr->qbr",
        root_select,
        mid_contrib.reshape(fronts, mid_width, BLOCK, scenarios),
        preferred_element_type=jnp.float32,
        precision=lax.Precision.HIGHEST,
    )
    root_start = root_rhs + root_added.reshape(root_width * BLOCK, scenarios)
    root_fwd = across_front(
        jnp.dot(
            root_lower,
            root_start,
            preferred_element_type=jnp.float32,
            precision=lax.Precision.HIGHEST,
        )
    )
    root_sol = across_subtree(
        jnp.dot(
            root_upper,
            root_fwd,
            preferred_element_type=jnp.float32,
            precision=lax.Precision.HIGHEST,
        )
    )
    mid_ext = jnp.einsum(
        "qpk,qbr->pkbr",
        root_select,
        root_sol.reshape(root_width, BLOCK, scenarios),
        preferred_element_type=jnp.float32,
        precision=lax.Precision.HIGHEST,
    )
    mid_ext = mid_ext.reshape(fronts, mid_width * BLOCK, scenarios)
    mid_back = mid_fwd - across_front(batched(mid_right, mid_ext))
    mid_sol = across_subtree(batched(mid_upper, mid_back))
    whole_column = jnp.stack(
        [
            mid_sol.reshape(fronts, mid_width, BLOCK, scenarios),
            mid_ext.reshape(fronts, mid_width, BLOCK, scenarios),
        ],
        axis=1,
    )
    leaf_ext = jnp.einsum(
        "phqgk,phqbr->gkbr",
        own_select,
        whole_column,
        preferred_element_type=jnp.float32,
        precision=lax.Precision.HIGHEST,
    )
    leaf_ext = leaf_ext.reshape(local_rows, scenarios)
    leaf_back = live * (leaf_fwd - leaf_product(leaf_right[0], leaf_ext))
    leaf_sol = live * leaf_product(leaf_upper[0], leaf_back)
    return (leaf_sol[None], mid_sol, root_sol)


def solution(mesh):
    return jax.shard_map(
        on_device,
        mesh=mesh,
        in_specs=(
            P("subtree", "front", None),
            P(None, "front", None),
            P("front", None),
            P("subtree", None, "front"),
            P("subtree", None, "front"),
            P("subtree", None, "front"),
            P("subtree", None, "front"),
            P(None, "subtree", "front"),
            P(None, "front", "subtree"),
            P(None, "subtree", "front"),
            P(None, "front", "subtree"),
            P("subtree", "front"),
            P("front", "subtree"),
            P(),
            P(),
            P(),
            P(),
        ),
        out_specs=(P("subtree", "front", None), P(None, "front", None), P("front", None)),
        check_vma=False,
    )
```

profile of v0, /device:TPU:0, one launch (start us, length us, event | category | flops | bytes accessed | tf_op | source)
XLA Modules:
  0.0 725.7 jit_solution(1965828273986753131)
XLA Ops:
  9.1 10.6 %fusion.15 = f32[2048,256]{0,1:T(8,128)} fusion(f32[1,2048,512]{2,1,0:T(8,128)} %param.20, f32[1,512,256]{2,1,0:T(8,128)} %param.17, f32[512]{0:T(512)S(1)} %fusion.57), kind=kOutput, calls=%fused_computation.16 | convolution fusion | flops 3221356544 | bytes 6817792 | tf_op jit(solution)/shard_map/dot_general | solution.py:12
  19.8 38.0 %reduce-scatter.5.cloned.1.call-done = f32[512,256]{0,1:T(8,128)} async-done(((f32[2048,256]{0,1:T(8,128)}), f32[512,256]{0,1:T(8,128)}) %reduce-scatter.5.cloned.1.call-update) | async-done | bytes 524304 | tf_op jit(solution)/shard_map/reduce_scatter | solution.py:11
  57.8 7.3 %fusion.18 = f32[2048,256]{0,1:T(8,128)} fusion(f32[1,2048,512]{2,1,0:T(8,128)} %param.21, f32[512,256]{0,1:T(8,128)} %reduce-scatter.5.cloned.1.call-done, f32[512]{0:T(512)S(1)} %fusion.57), kind=kOutput, calls=%fused_computation.17 | convolution fusion | flops 3221356544 | bytes 6817792 | tf_op jit(solution)/shard_map/dot_general | solution.py:12
  65.2 35.3 %reduce-scatter.7.cloned.1.call-done = f32[512,256]{0,1:T(8,128)} async-done(((f32[2048,256]{0,1:T(8,128)}), f32[512,256]{0,1:T(8,128)}) %reduce-scatter.7.cloned.1.call-update) | async-done | bytes 524304 | tf_op jit(solution)/shard_map/reduce_scatter | solution.py:11
  102.9 46.6 %all-gather.3.cloned.1.call-done = f32[4096,256]{0,1:T(8,128)} async-done(((f32[512,256]{0,1:T(8,128)}), f32[4096,256]{0,1:T(8,128)}) %all-gather.3.cloned.1.call-update) | async-done | bytes 4194320 | tf_op jit(solution)/shard_map/all_gather | solution.py:86
  149.5 6.0 reshape.127
  155.6 6.6 copy.48
  162.2 6.1 convolution_bitcast_fusion.2
  171.2 8.0 %fusion.29 = f32[2,512,256]{1,2,0:T(8,128)} fusion(f32[2,512,1024]{2,1,0:T(8,128)S(1)} %copy-done.2, f32[2,1024,256]{2,1,0:T(8,128)S(1)} %copy-done.6, f32[2,1024,256]{2,1,0:T(8,128)S(1)} %bitcast.122), kind=kOutput, calls=%fused_computation.28 | convolution fusion | flops 3221749760 | bytes 9437184 | tf_op jit(solution)/shard_map/fab,fbr->far/dot_general | solution.py:30
  179.4 51.2 %all-reduce.7.cloned.1.call-done = f32[2,512,256]{1,2,0:T(8,128)} async-done(((f32[2,512,256]{1,2,0:T(8,128)}), f32[2,512,256]{1,2,0:T(8,128)}) %all-reduce.7.cloned.1.call-update) | async-done | bytes 1048592 | tf_op jit(solution)/shard_map/psum | solution.py:22
  230.6 7.5 %convolution_bitcast_fusion.5 = f32[2,1024,256]{1,2,0:T(8,128)} fusion(f32[2,512,256]{1,2,0:T(8,128)} %all-reduce.7.cloned.1.call-done, f32[2,1024,512]{2,1,0:T(8,128)} %param.25), kind=kOutput, calls=%fused_computation.27 | convolution fusion | flops 3221225472 | bytes 7340032 | tf_op jit(solution)/shard_map/fab,fbr->far/dot_general | solution.py:30
  238.3 1.9 copy.33
  242.1 61.3 %all-reduce.9.cloned.1.call-done = f32[2,1024,256]{1,2,0:T(8,128)} async-done(((f32[2,1024,256]{1,2,0:T(8,128)}), f32[2,1024,256]{1,2,0:T(8,128)}) %all-reduce.9.cloned.1.call-update) | async-done | bytes 2097168 | tf_op jit(solution)/shard_map/psum | solution.py:26
  303.4 2.1 sub.9
  305.9 2.0 copy.35
  308.0 3.2 convolution_bitcast_fusion.3
  313.2 26.2 %convolution_bitcast_fusion.1 = f32[1280,256]{0,1:T(8,128)} fusion(f32[2560,256]{1,0:T(8,128)S(1)} %bitcast_add_fusion, f32[1280,2560]{1,0:T(8,128)} %param.28), kind=kOutput, calls=%fused_computation.20 | convolution fusion | flops 10066329600 | bytes 17039360 | tf_op jit(solution)/shard_map/dot_general | solution.py:111
  339.5 56.1 %all-reduce.11.cloned.1.call-done = f32[1280,256]{0,1:T(8,128)} async-done(((f32[1280,256]{0,1:T(8,128)}), f32[1280,256]{0,1:T(8,128)}) %all-reduce.11.cloned.1.call-update) | async-done | bytes 1310736 | tf_op jit(solution)/shard_map/psum | solution.py:22
  395.6 15.6 %convolution_bitcast_fusion = f32[2560,256]{0,1:T(8,128)} fusion(f32[1280,256]{0,1:T(8,128)} %all-reduce.11.cloned.1.call-done, f32[2560,1280]{1,0:T(8,128)} %param.29), kind=kOutput, calls=%fused_computation.12 | convolution fusion | flops 10066329600 | bytes 17039360 | tf_op jit(solution)/shard_map/dot_general | solution.py:119
  411.3 69.2 %all-reduce.13.cloned.1.call-done = f32[2560,256]{0,1:T(8,128)} async-done(((f32[2560,256]{0,1:T(8,128)}), f32[2560,256]{0,1:T(8,128)}) %all-reduce.13.cloned.1.call-update) | async-done | bytes 2621456 | tf_op jit(solution)/shard_map/psum | solution.py:26
  480.5 3.2 copy.37
  483.7 4.4 fusion.12
  490.3 8.0 %convolution_bitcast_fusion.6 = f32[2,512,256]{1,2,0:T(8,128)} fusion(f32[2,1024,256]{2,1,0:T(8,128)S(1)} %bitcast.118, f32[2,512,1024]{2,1,0:T(8,128)S(1)} %copy-done.1), kind=kOutput, calls=%fused_computation.29 | convolution fusion | flops 3221225472 | bytes 7340032 | tf_op jit(solution)/shard_map/fab,fbr->far/dot_general | solution.py:30
  498.6 51.4 %all-reduce.15.cloned.1.call-done = f32[2,512,256]{1,2,0:T(8,128)} async-done(((f32[2,512,256]{1,2,0:T(8,128)}), f32[2,512,256]{1,2,0:T(8,128)}) %all-reduce.15.cloned.1.call-update) | async-done | bytes 1048592 | tf_op jit(solution)/shard_map/psum | solution.py:22
  550.0 7.5 %convolution_bitcast_fusion.4 = f32[2,1024,256]{1,2,0:T(8,128)} fusion(f32[2,1024,512]{2,1,0:T(8,128)} %param.27, f32[2,512,256]{1,2,0:T(8,128)S(1)} %copy-done.4, f32[2,512,256]{1,2,0:T(8,128)} %all-reduce.15.cloned.1.call-done), kind=kOutput, calls=%fused_computation.26 | convolution fusion | flops 3221487616 | bytes 8388608 | tf_op jit(solution)/shard_map/fab,fbr->far/dot_general | solution.py:30
  559.0 63.8 %all-reduce.17.cloned.1.call-done = f32[2,1024,256]{1,2,0:T(8,128)} async-done(((f32[2,1024,256]{1,2,0:T(8,128)}), f32[2,1024,256]{1,2,0:T(8,128)}) %all-reduce.17.cloned.1.call-update) | async-done | bytes 2097168 | tf_op jit(solution)/shard_map/psum | solution.py:26
  622.8 2.9 copy.40
  625.6 2.8 copy.41
  630.6 8.4 %fusion.21 = f32[2048,256]{0,1:T(8,128)} fusion(f32[512,256]{1,0:T(8,128)S(1)} %bitcast.123, f32[1,2048,512]{2,1,0:T(8,128)S(1)} %copy-done.3), kind=kOutput, calls=%fused_computation.18 | convolution fusion | flops 3221225472 | bytes 6815744 | tf_op jit(solution)/shard_map/dot_general | solution.py:12
  639.3 34.6 %reduce-scatter.9.cloned.1.call-done = f32[512,256]{0,1:T(8,128)} async-done(((f32[2048,256]{0,1:T(8,128)}), f32[512,256]{0,1:T(8,128)}) %reduce-scatter.9.cloned.1.call-update) | async-done | bytes 524304 | tf_op jit(solution)/shard_map/reduce_scatter | solution.py:11
  674.0 7.4 %fusion.24 = f32[2048,256]{0,1:T(8,128)} fusion(f32[1,2048,512]{2,1,0:T(8,128)} %param.23, f32[512,256]{0,1:T(8,128)} %reduce-scatter.9.cloned.1.call-done, f32[512,256]{0,1:T(8,128)S(1)} %copy-done.7, f32[512]{0:T(512)S(1)} %fusion.57), kind=kOutput, calls=%fused_computation.19 | convolution fusion | flops 3221618688 | bytes 7342080 | tf_op jit(solution)/shard_map/dot_general | solution.py:12
  681.3 35.3 %reduce-scatter.11.cloned.1.call-done = f32[512,256]{0,1:T(8,128)} async-done(((f32[2048,256]{0,1:T(8,128)}), f32[512,256]{0,1:T(8,128)}) %reduce-scatter.11.cloned.1.call-update) | async-done | bytes 524304 | tf_op jit(solution)/shard_map/reduce_scatter | solution.py:11
  (68 shorter events, 20.8 us)
Async XLA Ops:
  7.2 95.4 %copy-start = (s32[8,16]{1,0:T(8,128)S(1)}, s32[8,16]{1,0:T(8,128)}, u32[]{:S(2)}) copy-start(s32[8,16]{1,0:T(8,128)} %param.32) | copy-start | bytes 1540
  7.2 50.6 %reduce-scatter.5.cloned.1.call-start = ((), (), s32[]{:S(2)}) async-start(), calls=%async_computation.4 | async-start | bytes 2621440 | tf_op jit(solution)/shard_map/reduce_scatter | solution.py:11
  19.7 80.7 %reduce-scatter.7.cloned.1.call-start = ((), (), s32[]{:S(2)}) async-start(), calls=%async_computation.5 | async-start | bytes 2621440 | tf_op jit(solution)/shard_map/reduce_scatter | solution.py:11
  65.1 37.7 %copy-start.9 = (s32[8]{0:T(128)S(1)}, s32[8]{0:T(128)}, u32[]{:S(2)}) copy-start(s32[8]{0:T(128)} %param.30) | copy-start | bytes 100
  65.1 84.4 %all-gather.3.cloned.1.call-start = ((), (), s32[]{:S(2)}) async-start(), calls=%async_computation.14 | async-start | bytes 4718592 | tf_op jit(solution)/shard_map/all_gather | solution.py:86
  102.4 128.2 %all-reduce.7.cloned.1.call-start = ((), (), s32[]{:S(2)}) async-start(), calls=%async_computation.6 | async-start | bytes 2097152 | tf_op jit(solution)/shard_map/psum | solution.py:22
  168.3 1.6 copy-start.6
  168.6 2.5 copy-start.2
  179.2 59.0 %copy-start.8 = (s32[2,32]{1,0:T(2,128)S(1)}, s32[2,32]{1,0:T(2,128)}, u32[]{:S(2)}) copy-start(s32[2,32]{1,0:T(2,128)} %param.33) | copy-start | bytes 772
  179.2 124.2 %all-reduce.9.cloned.1.call-start = ((), (), s32[]{:S(2)}) async-start(), calls=%async_computation.7 | async-start | bytes 4194304 | tf_op jit(solution)/shard_map/psum | solution.py:26
  238.1 157.4 %all-reduce.11.cloned.1.call-start = ((), (), s32[]{:S(2)}) async-start(), calls=%async_computation.8 | async-start | bytes 2621440 | tf_op jit(solution)/shard_map/psum | solution.py:22
  311.2 1.7 copy-start.5
  339.4 141.1 %all-reduce.13.cloned.1.call-start = ((), (), s32[]{:S(2)}) async-start(), calls=%async_computation.9 | async-start | bytes 5242880 | tf_op jit(solution)/shard_map/psum | solution.py:26
  411.2 138.8 %all-reduce.15.cloned.1.call-start = ((), (), s32[]{:S(2)}) async-start(), calls=%async_computation.10 | async-start | bytes 2097152 | tf_op jit(solution)/shard_map/psum | solution.py:22
  488.1 2.2 copy-start.1
  490.3 59.8 %copy-start.4 = (f32[2,512,256]{1,2,0:T(8,128)S(1)}, f32[2,512,256]{1,2,0:T(8,128)}, u32[]{:S(2)}) copy-start(f32[2,512,256]{1,2,0:T(8,128)} %all-reduce.7.cloned.1.call-done) | copy-start | bytes 3145732
  498.3 124.4 %all-reduce.17.cloned.1.call-start = ((), (), s32[]{:S(2)}) async-start(), calls=%async_computation.11 | async-start | bytes 4194304 | tf_op jit(solution)/shard_map/psum | solution.py:26
  557.5 116.4 %reduce-scatter.9.cloned.1.call-start = ((), (), s32[]{:S(2)}) async-start(), calls=%async_computation.12 | async-start | bytes 2621440 | tf_op jit(solution)/shard_map/reduce_scatter | solution.py:11
  628.5 2.2 copy-start.3
  630.6 43.3 %copy-start.7 = (f32[512,256]{0,1:T(8,128)S(1)}, f32[512,256]{0,1:T(8,128)}, u32[]{:S(2)}) copy-start(f32[512,256]{0,1:T(8,128)} %reduce-scatter.5.cloned.1.call-done) | copy-start | bytes 1572868
  639.0 77.7 %reduce-scatter.11.cloned.1.call-start = ((), (), s32[]{:S(2)}) async-start(), calls=%async_computation.13 | async-start | bytes 2621440 | tf_op jit(solution)/shard_map/reduce_scatter | solution.py:11
Sparse Core Ops, SparseCore 0:
  19.8 37.9 reduce-scatter.4
  65.2 35.1 reduce-scatter.6
  102.6 46.8 all-gather.2
  179.3 51.2 all-reduce.6
  238.2 65.1 all-reduce.8
  339.6 55.9 all-reduce.10
  411.3 69.0 all-reduce.12
  498.4 51.5 all-reduce.14
  557.6 65.0 all-reduce.16
  639.1 34.7 reduce-scatter.8
  681.5 35.1 reduce-scatter.10
where the time goes:
time: 734 us; the launch traced here: 726 us
  waiting for transfers between devices  543 us (74%)
  matrix products  122 us (17%)
  local copies, waits for them, and re-layouts  38.1 us (5%)
  between operations  14.5 us (2%)
    psum x3, waiting for transfers between devices, across_subtree(): return lax.psum(partial_value, 'subtree')  194 us
    psum x3, waiting for transfers between devices, across_front(): return lax.psum(partial_value, 'front')  159 us
    reduce_scatter x4, waiting for transfers between devices, leaf_product(): lax.psum_scatter(jnp.dot(matrix, vector, preferred_element_type=jnp.float...  143 us
    all_gather x1, waiting for transfers between devices, on_device(): piece = lax.all_gather(leaf_contrib[None], 'subtree', axis=0, tiled=True)  46.6 us
    dot_general x4, matrix products, leaf_product(): jnp.dot(matrix, vector, preferred_element_type=jnp.float32, precision=lax...  33.6 us
    dot_general x4, matrix products, batched(): jnp.einsum('fab,fbr->far', matrix, vector, preferred_element_type=jnp.flo...  31 us
    dot_general x1, matrix products, on_device(): jnp.dot(root_lower, root_start, preferred_element_type=jnp.float32, preci...  26.2 us
    dot_general x1, matrix products, on_device(): jnp.dot(root_upper, root_fwd, preferred_element_type=jnp.float32, precisi...  15.6 us
  transfers between devices with their start and end apart: 11, of which 11 were waited for; matrix products, arithmetic and copies ran while one was open for 1% of the time, Pallas kernels for 0%

commit v1 on v0

--- a/solution.py
+++ b/solution.py
@@ -5,6 +5,22 @@
 
 MID_PIV = 4096
 BLOCK = 128
+
+
+def frames_wait(array_in, axis_key):
+    k_all = lax.psum(1, axis_name=axis_key)
+    o_now = range(1, k_all)
+    d_next = list(map(lambda j0: (j0 - 1, j0), o_now))
+    formed = d_next + [(k_all - 1, 0)]
+    tmp = array_in
+    block_list = [tmp]
+    ix = 0
+    while ix < k_all - 1:
+        tmp = lax.ppermute(tmp, axis_name=axis_key, perm=formed)
+        block_list += [tmp]
+        ix = ix + 1
+    arr_now = jnp.concatenate([*reversed(block_list)], 0)
+    return jnp.roll(arr_now, (lax.axis_index(axis_key) + 1) * tmp.shape[0], axis=0)
 
 
 def leaf_product(matrix, vector):
@@ -83,7 +99,7 @@
     own_select = leaf_select(own_parent, own_blocks, fronts, column, mid_width)
     column_blocks = lax.dynamic_slice_in_dim(leaf_map, column * leaf_width, leaf_width, 1)
     selection = leaf_select(leaf_parent, column_blocks, fronts, column, mid_width)
-    piece = lax.all_gather(leaf_contrib[None], "subtree", axis=0, tiled=True)
+    piece = frames_wait(leaf_contrib[None], "subtree")
     shaped = piece.reshape(piece.shape[0], leaf_width, BLOCK, scenarios)
     assembled = jnp.einsum(
         "phqgk,gkbr->phqbr",

time: 734 us -> 759 us (1.034)
  waiting for transfers between devices: 543 us -> 568 us
    ppermute x0 -> x7, waiting for transfers between devices: none -> 72.8 us  [frames_wait(): tmp = lax.ppermute(tmp, axis_name=axis_key, perm=formed)]
    all_gather x1 -> x0, waiting for transfers between devices: 46.6 us -> none  [on_device(): piece = lax.all_gather(leaf_contrib[None], 'subtree', axis=0, tiled=True)]
    reshape x2 -> x0, local copies, waits for them, and re-layouts: 12.6 us -> none  [on_device(): shaped = piece.reshape(piece.shape[0], leaf_width, BLOCK, scenarios)]
    dynamic_slice x0 -> x2, local copies, waits for them, and re-layouts: none -> 8.28 us  [frames_wait(): jnp.roll(arr_now, (lax.axis_index(axis_key) + 1) * tmp.shape[0], axis=0)]
  transfers between devices with their start and end apart: 11 -> 17, of which waited for: 11 -> 17; matrix products, arithmetic and copies ran while one was open for 1% -> 1% of each run, Pallas kernels for 0% -> 0%
where the time goes in v1:
time: 759 us; the launch traced here: 749 us
  waiting for transfers between devices  568 us (75%)
  matrix products  125 us (16%)
  local copies, waits for them, and re-layouts  34.8 us (5%)
  between operations  15 us (2%)
    psum x3, waiting for transfers between devices, across_subtree(): return lax.psum(partial_value, 'subtree')  194 us
    psum x3, waiting for transfers between devices, across_front(): return lax.psum(partial_value, 'front')  157 us
    reduce_scatter x4, waiting for transfers between devices, leaf_product(): lax.psum_scatter(jnp.dot(matrix, vector, preferred_element_type=jnp.float...  143 us
    ppermute x7, waiting for transfers between devices, frames_wait(): tmp = lax.ppermute(tmp, axis_name=axis_key, perm=formed)  72.8 us
    dot_general x4, matrix products, leaf_product(): jnp.dot(matrix, vector, preferred_element_type=jnp.float32, precision=lax...  33.6 us
    dot_general x4, matrix products, batched(): jnp.einsum('fab,fbr->far', matrix, vector, preferred_element_type=jnp.flo...  31.2 us
    dot_general x1, matrix products, on_device(): jnp.dot(root_lower, root_start, preferred_element_type=jnp.float32, preci...  26.2 us
    dot_general x1, matrix products, on_device(): jnp.dot(root_upper, root_fwd, preferred_element_type=jnp.float32, precisi...  15.6 us
  transfers between devices with their start and end apart: 17, of which 17 were waited for; matrix products, arithmetic and copies ran while one was open for 1% of the time, Pallas kernels for 0%

profile of v1, /device:TPU:0, one launch (start us, length us, event | category | flops | bytes accessed | tf_op | source)
XLA Modules:
  0.0 749.2 jit_solution(12197424802115103946)
XLA Ops:
  9.1 10.6 %fusion.17 = f32[2048,256]{0,1:T(8,128)} fusion(f32[1,2048,512]{2,1,0:T(8,128)} %param.20, f32[1,512,256]{2,1,0:T(8,128)} %param.17, f32[512]{0:T(512)S(1)} %fusion.62), kind=kOutput, calls=%fused_computation.18 | convolution fusion | flops 3221356544 | bytes 6817792 | tf_op jit(solution)/shard_map/dot_general | solution.py:28
  19.8 38.0 %reduce-scatter.5.cloned.1.call-done = f32[512,256]{0,1:T(8,128)} async-done(((f32[2048,256]{0,1:T(8,128)}), f32[512,256]{0,1:T(8,128)}) %reduce-scatter.5.cloned.1.call-update) | async-done | bytes 524304 | tf_op jit(solution)/shard_map/reduce_scatter | solution.py:27
  57.8 7.3 fusion.20
  65.2 35.3 %reduce-scatter.7.cloned.1.call-done = f32[512,256]{0,1:T(8,128)} async-done(((f32[2048,256]{0,1:T(8,128)}), f32[512,256]{0,1:T(8,128)}) %reduce-scatter.7.cloned.1.call-update) | async-done | bytes 524304 | tf_op jit(solution)/shard_map/reduce_scatter | solution.py:27
  101.7 10.4 %collective-permute-done = f32[1,512,256]{1,2,0:T(8,128)S(1)} collective-permute-done((f32[1,512,256]{1,2,0:T(8,128)S(1)}, f32[1,512,256]{1,2,0:T(8,128)S(1)}, u32[]{:S(2)}, u32[]{:S(2)}) %collective-permute-start) | collective-permute-done | bytes 524320 | tf_op jit(solution)/shard_map/ppermute | solution.py:19
  112.1 10.4 %collective-permute-done.1 = f32[1,512,256]{1,2,0:T(8,128)S(1)} collective-permute-done((f32[1,512,256]{1,2,0:T(8,128)S(1)}, f32[1,512,256]{1,2,0:T(8,128)S(1)}, u32[]{:S(2)}, u32[]{:S(2)}) %collective-permute-start.1) | collective-permute-done | bytes 524320 | tf_op jit(solution)/shard_map/ppermute | solution.py:19
  122.5 10.4 %collective-permute-done.2 = f32[1,512,256]{1,2,0:T(8,128)S(1)} collective-permute-done((f32[1,512,256]{1,2,0:T(8,128)S(1)}, f32[1,512,256]{1,2,0:T(8,128)S(1)}, u32[]{:S(2)}, u32[]{:S(2)}) %collective-permute-start.2) | collective-permute-done | bytes 524320 | tf_op jit(solution)/shard_map/ppermute | solution.py:19
  132.9 10.4 %collective-permute-done.3 = f32[1,512,256]{1,2,0:T(8,128)S(1)} collective-permute-done((f32[1,512,256]{1,2,0:T(8,128)S(1)}, f32[1,512,256]{1,2,0:T(8,128)S(1)}, u32[]{:S(2)}, u32[]{:S(2)}) %collective-permute-start.3) | collective-permute-done | bytes 524320 | tf_op jit(solution)/shard_map/ppermute | solution.py:19
  143.3 10.4 %collective-permute-done.4 = f32[1,512,256]{1,2,0:T(8,128)S(1)} collective-permute-done((f32[1,512,256]{1,2,0:T(8,128)S(1)}, f32[1,512,256]{1,2,0:T(8,128)S(1)}, u32[]{:S(2)}, u32[]{:S(2)}) %collective-permute-start.4) | collective-permute-done | bytes 524320 | tf_op jit(solution)/shard_map/ppermute | solution.py:19
  153.9 10.3 %collective-permute-done.5 = f32[1,512,256]{1,2,0:T(8,128)} collective-permute-done((f32[1,512,256]{1,2,0:T(8,128)S(1)}, f32[1,512,256]{1,2,0:T(8,128)}, u32[]{:S(2)}, u32[]{:S(2)}) %collective-permute-start.5) | collective-permute-done | bytes 524320 | tf_op jit(solution)/shard_map/ppermute | solution.py:19
  164.4 10.5 %collective-permute-done.6 = f32[1,512,256]{1,2,0:T(8,128)S(1)} collective-permute-done((f32[1,512,256]{1,2,0:T(8,128)}, f32[1,512,256]{1,2,0:T(8,128)S(1)}, u32[]{:S(2)}, u32[]{:S(2)}) %collective-permute-start.6) | collective-permute-done | bytes 524320 | tf_op jit(solution)/shard_map/ppermute | solution.py:19
  180.3 5.6 copy.29
  185.9 8.3 %fusion.29 = f32[2,2,8,128,256]{4,2,3,1,0:T(8,128)S(1)} fusion(f32[8,4,128,256,1,1]{3,2,1,0,5,4:T(8,128)} %bitcast.120, pred[2,8,8,4]{2,1,3,0:T(8,128)(4,1)S(1)} %broadcast_compare_fusion, pred[2,8]{1,0:T(4,128)(4,1)S(1)} %iota_compare_fusion), kind=kOutput, calls=%fused_computation.24 | convolution fusion | flops 402654208 | bytes 8389136 | tf_op jit(solution)/shard_map/phqgk,gkbr->phqbr/dot_general | solution.py:104
  197.2 8.2 %fusion.34 = f32[2,512,256]{1,2,0:T(8,128)} fusion(f32[2,512,1024]{2,1,0:T(8,128)S(1)} %copy-done.3, f32[2,1024,256]{2,1,0:T(8,128)S(1)} %copy-done.7, f32[2,1024,256]{2,1,0:T(8,128)S(1)} %bitcast.127), kind=kOutput, calls=%fused_computation.30 | convolution fusion | flops 3221749760 | bytes 9437184 | tf_op jit(solution)/shard_map/fab,fbr->far/dot_general | solution.py:46
  205.4 49.8 %all-reduce.7.cloned.1.call-done = f32[2,512,256]{1,2,0:T(8,128)} async-done(((f32[2,512,256]{1,2,0:T(8,128)}), f32[2,512,256]{1,2,0:T(8,128)}) %all-reduce.7.cloned.1.call-update) | async-done | bytes 1048592 | tf_op jit(solution)/shard_map/psum | solution.py:38
  255.2 7.5 convolution_bitcast_fusion.4
  266.7 61.2 %all-reduce.9.cloned.1.call-done = f32[2,1024,256]{1,2,0:T(8,128)} async-done(((f32[2,1024,256]{1,2,0:T(8,128)}), f32[2,1024,256]{1,2,0:T(8,128)}) %all-reduce.9.cloned.1.call-update) | async-done | bytes 2097168 | tf_op jit(solution)/shard_map/psum | solution.py:42
  332.5 3.2 convolution_bitcast_fusion.2
  337.8 26.2 %convolution_bitcast_fusion.1 = f32[1280,256]{0,1:T(8,128)} fusion(f32[2560,256]{1,0:T(8,128)S(1)} %bitcast_add_fusion, f32[1280,2560]{1,0:T(8,128)} %param.28), kind=kOutput, calls=%fused_computation.22 | convolution fusion | flops 10066329600 | bytes 17039360 | tf_op jit(solution)/shard_map/dot_general | solution.py:127
  364.1 56.1 %all-reduce.11.cloned.1.call-done = f32[1280,256]{0,1:T(8,128)} async-done(((f32[1280,256]{0,1:T(8,128)}), f32[1280,256]{0,1:T(8,128)}) %all-reduce.11.cloned.1.call-update) | async-done | bytes 1310736 | tf_op jit(solution)/shard_map/psum | solution.py:38
  420.2 15.6 %convolution_bitcast_fusion = f32[2560,256]{0,1:T(8,128)} fusion(f32[1280,256]{0,1:T(8,128)} %all-reduce.11.cloned.1.call-done, f32[2560,1280]{1,0:T(8,128)} %param.29), kind=kOutput, calls=%fused_computation.14 | convolution fusion | flops 10066329600 | bytes 17039360 | tf_op jit(solution)/shard_map/dot_general | solution.py:135
  435.9 69.2 %all-reduce.13.cloned.1.call-done = f32[2560,256]{0,1:T(8,128)} async-done(((f32[2560,256]{0,1:T(8,128)}), f32[2560,256]{0,1:T(8,128)}) %all-reduce.13.cloned.1.call-update) | async-done | bytes 2621456 | tf_op jit(solution)/shard_map/psum | solution.py:42
  505.0 3.2 copy.37
  508.3 4.5 fusion.14
  513.4 8.0 %convolution_bitcast_fusion.5 = f32[2,512,256]{1,2,0:T(8,128)} fusion(f32[2,1024,256]{2,1,0:T(8,128)S(1)} %bitcast.123, f32[2,512,1024]{2,1,0:T(8,128)S(1)} %copy-done.2), kind=kOutput, calls=%fused_computation.31 | convolution fusion | flops 3221225472 | bytes 7340032 | tf_op jit(solution)/shard_map/fab,fbr->far/dot_general | solution.py:46
  521.8 51.4 %all-reduce.15.cloned.1.call-done = f32[2,512,256]{1,2,0:T(8,128)} async-done(((f32[2,512,256]{1,2,0:T(8,128)}), f32[2,512,256]{1,2,0:T(8,128)}) %all-reduce.15.cloned.1.call-update) | async-done | bytes 1048592 | tf_op jit(solution)/shard_map/psum | solution.py:38
  573.2 7.5 convolution_bitcast_fusion.3
  582.1 63.8 %all-reduce.17.cloned.1.call-done = f32[2,1024,256]{1,2,0:T(8,128)} async-done(((f32[2,1024,256]{1,2,0:T(8,128)}), f32[2,1024,256]{1,2,0:T(8,128)}) %all-reduce.17.cloned.1.call-update) | async-done | bytes 2097168 | tf_op jit(solution)/shard_map/psum | solution.py:42
  653.8 8.4 %fusion.23 = f32[2048,256]{0,1:T(8,128)} fusion(f32[512,256]{1,0:T(8,128)S(1)} %bitcast.128, f32[1,2048,512]{2,1,0:T(8,128)S(1)} %copy-done.4), kind=kOutput, calls=%fused_computation.20 | convolution fusion | flops 3221225472 | bytes 6815744 | tf_op jit(solution)/shard_map/dot_general | solution.py:28
  662.5 34.6 %reduce-scatter.9.cloned.1.call-done = f32[512,256]{0,1:T(8,128)} async-done(((f32[2048,256]{0,1:T(8,128)}), f32[512,256]{0,1:T(8,128)}) %reduce-scatter.9.cloned.1.call-update) | async-done | bytes 524304 | tf_op jit(solution)/shard_map/reduce_scatter | solution.py:27
  697.1 7.4 fusion.26
  704.5 35.3 %reduce-scatter.11.cloned.1.call-done = f32[512,256]{0,1:T(8,128)} async-done(((f32[2048,256]{0,1:T(8,128)}), f32[512,256]{0,1:T(8,128)}) %reduce-scatter.11.cloned.1.call-update) | async-done | bytes 524304 | tf_op jit(solution)/shard_map/reduce_scatter | solution.py:27
  (97 shorter events, 35.3 us)
Async XLA Ops:
  7.2 146.5 %copy-start = (s32[8,16]{1,0:T(8,128)S(1)}, s32[8,16]{1,0:T(8,128)}, u32[]{:S(2)}) copy-start(s32[8,16]{1,0:T(8,128)} %param.32) | copy-start | bytes 1540
  7.2 50.6 %reduce-scatter.5.cloned.1.call-start = ((), (), s32[]{:S(2)}) async-start(), calls=%async_computation.4 | async-start | bytes 2621440 | tf_op jit(solution)/shard_map/reduce_scatter | solution.py:27
  19.7 134.1 %copy-start.10 = (s32[8]{0:T(128)S(1)}, s32[8]{0:T(128)}, u32[]{:S(2)}) copy-start(s32[8]{0:T(128)} %param.30) | copy-start | bytes 100
  19.7 80.7 %reduce-scatter.7.cloned.1.call-start = ((), (), s32[]{:S(2)}) async-start(), calls=%async_computation.5 | async-start | bytes 2621440 | tf_op jit(solution)/shard_map/reduce_scatter | solution.py:27
  65.1 190.1 %all-reduce.7.cloned.1.call-start = ((), (), s32[]{:S(2)}) async-start(), calls=%async_computation.6 | async-start | bytes 2097152 | tf_op jit(solution)/shard_map/psum | solution.py:38
  100.5 75.7 %copy-start.1 = (f32[512,256]{0,1:T(8,128)S(1)}, f32[512,256]{0,1:T(8,128)}, u32[]{:S(2)}) copy-start(f32[512,256]{0,1:T(8,128)} %reduce-scatter.7.cloned.1.call-done) | copy-start | bytes 1572868
  101.6 10.5 %collective-permute-start = (f32[1,512,256]{1,2,0:T(8,128)S(1)}, f32[1,512,256]{1,2,0:T(8,128)S(1)}, u32[]{:S(2)}, u32[]{:S(2)}) collective-permute-start(f32[1,512,256]{1,2,0:T(8,128)S(1)} %negate_bitcast_fusion), channel_id=1, source_target_pairs={{0,4},{4,8},{8,12},{12,16},{16,20},{20,24},{24,28},{28,0},{1,5},{5... | collective-permute-start | bytes 1572872 | tf_op jit(solution)/shard_map/ppermute | solution.py:19
  112.1 10.4 %collective-permute-start.1 = (f32[1,512,256]{1,2,0:T(8,128)S(1)}, f32[1,512,256]{1,2,0:T(8,128)S(1)}, u32[]{:S(2)}, u32[]{:S(2)}) collective-permute-start(f32[1,512,256]{1,2,0:T(8,128)S(1)} %collective-permute-done), channel_id=1, source_target_pairs={{0,4},{4,8},{8,12},{12,16},{16,20},{20,24},{24,28},{28,0},{1,5},{5... | collective-permute-start | bytes 1572872 | tf_op jit(solution)/shard_map/ppermute | solution.py:19
  122.5 10.4 %collective-permute-start.2 = (f32[1,512,256]{1,2,0:T(8,128)S(1)}, f32[1,512,256]{1,2,0:T(8,128)S(1)}, u32[]{:S(2)}, u32[]{:S(2)}) collective-permute-start(f32[1,512,256]{1,2,0:T(8,128)S(1)} %collective-permute-done.1), channel_id=1, source_target_pairs={{0,4},{4,8},{8,12},{12,16},{16,20},{20,24},{24,28},{28,0},{1,5},{5... | collective-permute-start | bytes 1572872 | tf_op jit(solution)/shard_map/ppermute | solution.py:19
  132.9 10.4 %collective-permute-start.3 = (f32[1,512,256]{1,2,0:T(8,128)S(1)}, f32[1,512,256]{1,2,0:T(8,128)S(1)}, u32[]{:S(2)}, u32[]{:S(2)}) collective-permute-start(f32[1,512,256]{1,2,0:T(8,128)S(1)} %collective-permute-done.2), channel_id=1, source_target_pairs={{0,4},{4,8},{8,12},{12,16},{16,20},{20,24},{24,28},{28,0},{1,5},{5... | collective-permute-start | bytes 1572872 | tf_op jit(solution)/shard_map/ppermute | solution.py:19
  143.3 10.4 %collective-permute-start.4 = (f32[1,512,256]{1,2,0:T(8,128)S(1)}, f32[1,512,256]{1,2,0:T(8,128)S(1)}, u32[]{:S(2)}, u32[]{:S(2)}) collective-permute-start(f32[1,512,256]{1,2,0:T(8,128)S(1)} %collective-permute-done.3), channel_id=1, source_target_pairs={{0,4},{4,8},{8,12},{12,16},{16,20},{20,24},{24,28},{28,0},{1,5},{5... | collective-permute-start | bytes 1572872 | tf_op jit(solution)/shard_map/ppermute | solution.py:19
  153.7 10.5 %collective-permute-start.5 = (f32[1,512,256]{1,2,0:T(8,128)S(1)}, f32[1,512,256]{1,2,0:T(8,128)}, u32[]{:S(2)}, u32[]{:S(2)}) collective-permute-start(f32[1,512,256]{1,2,0:T(8,128)S(1)} %collective-permute-done.4), channel_id=1, source_target_pairs={{0,4},{4,8},{8,12},{12,16},{16,20},{20,24},{24,28},{28,0},{1,5},{5... | collective-permute-start | bytes 1572872 | tf_op jit(solution)/shard_map/ppermute | solution.py:19
  164.2 10.6 %collective-permute-start.6 = (f32[1,512,256]{1,2,0:T(8,128)}, f32[1,512,256]{1,2,0:T(8,128)S(1)}, u32[]{:S(2)}, u32[]{:S(2)}) collective-permute-start(f32[1,512,256]{1,2,0:T(8,128)} %collective-permute-done.5), channel_id=1, source_target_pairs={{0,4},{4,8},{8,12},{12,16},{16,20},{20,24},{24,28},{28,0},{1,5},{5... | collective-permute-start | bytes 1572872 | tf_op jit(solution)/shard_map/ppermute | solution.py:19
  194.2 1.6 copy-start.7
  194.6 2.5 copy-start.3
  205.4 57.4 %copy-start.9 = (s32[2,32]{1,0:T(2,128)S(1)}, s32[2,32]{1,0:T(2,128)}, u32[]{:S(2)}) copy-start(s32[2,32]{1,0:T(2,128)} %param.33) | copy-start | bytes 772
  205.4 122.6 %all-reduce.9.cloned.1.call-start = ((), (), s32[]{:S(2)}) async-start(), calls=%async_computation.7 | async-start | bytes 4194304 | tf_op jit(solution)/shard_map/psum | solution.py:42
  262.7 157.5 %all-reduce.11.cloned.1.call-start = ((), (), s32[]{:S(2)}) async-start(), calls=%async_computation.8 | async-start | bytes 2621440 | tf_op jit(solution)/shard_map/psum | solution.py:38
  335.7 1.7 copy-start.6
  364.0 141.0 %all-reduce.13.cloned.1.call-start = ((), (), s32[]{:S(2)}) async-start(), calls=%async_computation.9 | async-start | bytes 5242880 | tf_op jit(solution)/shard_map/psum | solution.py:42
  435.8 137.4 %all-reduce.15.cloned.1.call-start = ((), (), s32[]{:S(2)}) async-start(), calls=%async_computation.10 | async-start | bytes 2097152 | tf_op jit(solution)/shard_map/psum | solution.py:38
  508.3 5.2 copy-start.2
  513.4 59.8 %copy-start.5 = (f32[2,512,256]{1,2,0:T(8,128)S(1)}, f32[2,512,256]{1,2,0:T(8,128)}, u32[]{:S(2)}) copy-start(f32[2,512,256]{1,2,0:T(8,128)} %all-reduce.7.cloned.1.call-done) | copy-start | bytes 3145732
  521.5 124.4 %all-reduce.17.cloned.1.call-start = ((), (), s32[]{:S(2)}) async-start(), calls=%async_computation.11 | async-start | bytes 4194304 | tf_op jit(solution)/shard_map/psum | solution.py:42
  580.7 116.5 %reduce-scatter.9.cloned.1.call-start = ((), (), s32[]{:S(2)}) async-start(), calls=%async_computation.12 | async-start | bytes 2621440 | tf_op jit(solution)/shard_map/reduce_scatter | solution.py:27
  648.8 5.0 copy-start.4
  653.8 43.3 %copy-start.8 = (f32[512,256]{0,1:T(8,128)S(1)}, f32[512,256]{0,1:T(8,128)}, u32[]{:S(2)}) copy-start(f32[512,256]{0,1:T(8,128)} %reduce-scatter.5.cloned.1.call-done) | copy-start | bytes 1572868
  662.2 77.7 %reduce-scatter.11.cloned.1.call-start = ((), (), s32[]{:S(2)}) async-start(), calls=%async_computation.13 | async-start | bytes 2621440 | tf_op jit(solution)/shard_map/reduce_scatter | solution.py:27
Sparse Core Ops, SparseCore 0:
  19.8 37.9 reduce-scatter.4
  65.2 35.1 reduce-scatter.6
  205.5 49.6 all-reduce.6
  262.8 65.0 all-reduce.8
  364.2 55.9 all-reduce.10
  436.0 69.0 all-reduce.12
  521.6 51.5 all-reduce.14
  580.8 65.0 all-reduce.16
  662.3 34.7 reduce-scatter.8
  704.6 35.1 reduce-scatter.10
